TPU v7x, 256 devices: a whole 4x4x8 slice. The times are simulated.
256 devices in a mesh: dp: 8 (over y, core), ctx: 32 (over x, z).
Axes of the slice: x: 4, y: 4, z: 8, core: 2. Of those that a mesh axis runs over, the one named last changes fastest.
Arguments:
- query_rows: bfloat16 [8, 16384, 1024], P('dp', 'ctx'), may hold values from -6 to 6
- key_rows: bfloat16 [8, 16384, 1024], P('dp', 'ctx'), may hold values from -6 to 6
- value_rows: bfloat16 [8, 16384, 1024], P('dp', 'ctx'), may hold values from -6 to 6
- query_gain: float32 [128], replicated, may hold values from 0.5 to 1.5
- key_gain: float32 [128], replicated, may hold values from 0.5 to 1.5
- selected: int32 [8, 32, 3], P('dp', 'ctx'), may hold values from 0 to 30, as said below
- output_grad: bfloat16 [8, 16384, 1024], P('dp', 'ctx'), may hold values from -6 to 6
Outputs:
- attended: bfloat16 [8, 16384, 1024], P('dp', 'ctx')
- query_grad: bfloat16 [8, 16384, 1024], P('dp', 'ctx')
- key_grad: bfloat16 [8, 16384, 1024], P('dp', 'ctx')
- value_grad: bfloat16 [8, 16384, 1024], P('dp', 'ctx')
- query_gain_grad: float32 [128], replicated
- key_gain_grad: float32 [128], replicated
Inputs may be any that keep to these rules, and one draw needn't show every extreme that they name: selected[b, i, 0] is 0 for every query block i, and selected[b, i, 2] is i - 1 for every i >= 2. Every entry of row i lies in 0 to i, and an entry equal to i names no block. Entries below i are distinct within a row. For i >= 3 every entry is below i.
All inputs are finite; a program needn't handle non-finite values.
Results may differ from a plain program's by a relative error of at most 0.012.
Values may be sent and summed in bfloat16 or wider, within the bound.
A program may use at most 128 MiB of HBM per device.

v0:
```python
import jax
import jax.numpy as jnp
from jax import lax
from jax.sharding import PartitionSpec as P


def head_norm(inputs, gain_vector):
    head_dim = gain_vector.shape[0]
    shaped = inputs.reshape(inputs.shape[:-1] + (inputs.shape[-1] // head_dim, head_dim))
    factor = lax.rsqrt(jnp.mean(shaped * shaped, axis=-1, keepdims=True) + 1e-06)
    return (shaped * factor * gain_vector).reshape(inputs.shape)


def attend(query_block, key_list, value_list, visible_list, grad_block, score_scale):
    weight_list = []
    row_total = 0.0
    for key_block, visible in zip(key_list, visible_list):
        scores = jnp.einsum(
            "qhd,khd->hqk", query_block, key_block, preferred_element_type=jnp.float32
        )
        weights = jnp.exp(score_scale * scores) * visible
        row_total = row_total + jnp.sum(weights, axis=-1)
        weight_list.append(weights)
    prob_list = [(weights / row_total[:, :, None]).astype(jnp.bfloat16) for weights in weight_list]
    accumulated = 0.0
    for prob_block, value_block in zip(prob_list, value_list):
        accumulated = accumulated + jnp.einsum(
            "hqk,khd->qhd", prob_block, value_block, preferred_element_type=jnp.float32
        )
    output = accumulated.astype(jnp.bfloat16)
    row_delta = jnp.einsum("qhd,qhd->hq", grad_block, output, preferred_element_type=jnp.float32)
    query_grad = 0.0
    key_terms = []
    value_terms = []
    for prob_block, key_block, value_block in zip(prob_list, key_list, value_list):
        grad_probs = jnp.einsum(
            "qhd,khd->hqk", grad_block, value_block, preferred_element_type=jnp.float32
        )
        grad_scores = (
            prob_block.astype(jnp.float32) * (grad_probs - row_delta[:, :, None])
        ).astype(jnp.bfloat16)
        value_terms.append(
            jnp.einsum("hqk,qhd->khd", prob_block, grad_block, preferred_element_type=jnp.float32)
        )
        key_terms.append(
            score_scale
            * jnp.einsum(
                "hqk,qhd->khd", grad_scores, query_block, preferred_element_type=jnp.float32
            )
        )
        query_grad = query_grad + score_scale * jnp.einsum(
            "hqk,khd->qhd", grad_scores, key_block, preferred_element_type=jnp.float32
        )
    return (output, query_grad, key_terms, value_terms)


def local(query_rows, key_rows, value_rows, query_gain, key_gain, selected, output_grad):
    ctx_count = lax.axis_size("ctx")
    device_index = lax.axis_index("ctx")
    local_count = selected.shape[1]
    slot_total = selected.shape[2]
    token_count = query_rows.shape[1]
    model_width = query_rows.shape[2]
    head_dim = query_gain.shape[0]
    head_count = model_width // head_dim
    block_size = token_count // local_count
    slice_rows = block_size // ctx_count
    block_count = local_count * ctx_count
    score_scale = head_dim ** (-0.5)

    def heads_view(block_array):
        return block_array.reshape(block_size, head_count, head_dim)

    choice_table = lax.all_gather(selected[0], "ctx", axis=0, tiled=True)
    query_float = query_rows[0].astype(jnp.float32)
    key_float = key_rows[0].astype(jnp.float32)
    query_normed = head_norm(query_float, query_gain).astype(jnp.bfloat16)
    key_normed = head_norm(key_float, key_gain).astype(jnp.bfloat16)
    value_local = value_rows[0]
    holder_keys, holder_values = (
        lax.all_to_all(
            key_normed.reshape(local_count, block_size, model_width),
            "ctx",
            split_axis=1,
            concat_axis=0,
            tiled=True,
        ),
        lax.all_to_all(
            value_local.reshape(local_count, block_size, model_width),
            "ctx",
            split_axis=1,
            concat_axis=0,
            tiled=True,
        ),
    )
    first_slot = 0
    fetched_keys, fetched_values = (
        lax.all_to_all(holder_keys[choice_table], "ctx", split_axis=0, concat_axis=2, tiled=True),
        lax.all_to_all(holder_values[choice_table], "ctx", split_axis=0, concat_axis=2, tiled=True),
    )
    positions = jnp.arange(block_size)
    causal = (positions[None, :] <= positions[:, None]).astype(jnp.float32)[None]
    own_block = device_index * local_count + 0
    chosen = selected[0, 0]
    key_list = [heads_view(key_normed)]
    value_list = [heads_view(value_local)]
    visible_list = [causal]
    for slot_index in range(slot_total):
        fetched_slot = slot_index - first_slot
        key_list.append(heads_view(fetched_keys[0, fetched_slot]))
        value_list.append(heads_view(fetched_values[0, fetched_slot]))
        visible_list.append((chosen[slot_index] != own_block).astype(jnp.float32))
    output, query_grad, key_terms, value_terms = attend(
        heads_view(query_normed),
        key_list,
        value_list,
        visible_list,
        heads_view(output_grad[0, 0:block_size]),
        score_scale,
    )
    outputs = output.reshape(block_size, model_width)
    query_grads = query_grad.reshape(block_size, model_width)
    own_keys = [key_terms[0].reshape(block_size, model_width)]
    own_values = [value_terms[0].reshape(block_size, model_width)]
    remote_keys = [
        jnp.stack([grad_term.astype(jnp.bfloat16) for grad_term in key_terms[1:]]).reshape(
            slot_total, block_size, model_width
        )
    ]
    remote_values = [
        jnp.stack([grad_term.astype(jnp.bfloat16) for grad_term in value_terms[1:]]).reshape(
            slot_total, block_size, model_width
        )
    ]
    remote_key_all = jnp.stack(remote_keys)
    remote_value_all = jnp.stack(remote_values)
    back_keys, back_values = (
        lax.all_to_all(remote_key_all, "ctx", split_axis=2, concat_axis=0, tiled=True),
        lax.all_to_all(remote_value_all, "ctx", split_axis=2, concat_axis=0, tiled=True),
    )
    selector = (choice_table.reshape(-1)[None, :] == jnp.arange(block_count)[:, None]).astype(
        jnp.bfloat16
    )
    summed_keys = jnp.dot(
        selector,
        back_keys.reshape(block_count * slot_total, slice_rows * model_width),
        preferred_element_type=jnp.float32,
    )
    summed_values = jnp.dot(
        selector,
        back_values.reshape(block_count * slot_total, slice_rows * model_width),
        preferred_element_type=jnp.float32,
    )
    summed_keys = summed_keys.reshape(block_count, slice_rows, model_width)
    summed_values = summed_values.reshape(block_count, slice_rows, model_width)
    collected_keys, collected_values = (
        lax.all_to_all(
            summed_keys.astype(jnp.bfloat16), "ctx", split_axis=0, concat_axis=1, tiled=True
        ),
        lax.all_to_all(
            summed_values.astype(jnp.bfloat16), "ctx", split_axis=0, concat_axis=1, tiled=True
        ),
    )
    remote_key_total = collected_keys.astype(jnp.float32)
    remote_value_total = collected_values.astype(jnp.float32)
    key_total = (jnp.stack(own_keys) + remote_key_total).reshape(token_count, model_width)
    value_grad = (
        (jnp.stack(own_values) + remote_value_total)
        .reshape(token_count, model_width)
        .astype(jnp.bfloat16)
    )
    _, query_pull = jax.vjp(head_norm, query_float, query_gain)
    query_grad, query_gain_part = query_pull(query_grads)
    _, key_pull = jax.vjp(head_norm, key_float, key_gain)
    key_grad, key_gain_part = key_pull(key_total)
    query_gain_grad, key_gain_grad = lax.psum((query_gain_part, key_gain_part), ("dp", "ctx"))
    return (
        outputs[None],
        query_grad.astype(jnp.bfloat16)[None],
        key_grad.astype(jnp.bfloat16)[None],
        value_grad[None],
        query_gain_grad,
        key_gain_grad,
    )


def solution(mesh):
    in_specs = (
        P("dp", "ctx", None),
        P("dp", "ctx", None),
        P("dp", "ctx", None),
        P(),
        P(),
        P("dp", "ctx", None),
        P("dp", "ctx", None),
    )
    out_specs = (
        P("dp", "ctx", None),
        P("dp", "ctx", None),
        P("dp", "ctx", None),
        P("dp", "ctx", None),
        P(),
        P(),
    )
    return jax.shard_map(local, mesh=mesh, in_specs=in_specs, out_specs=out_specs, check_vma=False)
```

profile of v0, /device:TPU:1, one launch (start us, length us, event | category | flops | bytes accessed | tf_op | source)
XLA Modules:
  0.0 716.8 jit_solution(10691990284044521353)
XLA Ops:
  4.9 2.9 copy.602
  9.8 3.0 copy.640
  13.3 9.1 %reduce.7 = bf16[512,1024]{1,0:T(8,128)(2,1)} reduce(bf16[512,1,1024]{2,1,0:T(2,128)(2,1)} %bitcast.237, bf16[]{:T(256)} %broadcast.153), dimensions={1}, to_apply=%bitcast.200.reduce_sub_computation | reduce | bytes 2097154
  22.4 2.6 reshape.270
  25.0 12.2 %all-to-all-start = ((bf16[32,2,8192]{2,1,0:T(2,128)(2,1)}), bf16[32,2,8192]{2,1,0:T(2,128)(2,1)}, u32[]{:S(2)}, u32[]{:S(2)}) async-start(bf16[32,2,8192]{2,1,0:T(2,128)(2,1)} %reshape.270), calls=%async_computation | async-start | bytes 2097152 | tf_op jit(solution)/shard_map/all_to_all | solution.py:81
  37.1 3.0 copy.639
  40.1 8.0 %reduce.6 = bf16[512,1024]{1,0:T(8,128)(2,1)S(1)} reduce(bf16[512,1,1024]{2,1,0:T(2,128)(2,1)} %bitcast.238, bf16[]{:T(256)} %broadcast.153), dimensions={1}, to_apply=%bitcast.199.reduce_sub_computation | reduce | bytes 2097154
  49.7 12.0 %all-to-all-done = bf16[32,2,8192]{2,1,0:T(2,128)(2,1)} async-done(((bf16[32,2,8192]{2,1,0:T(2,128)(2,1)}), bf16[32,2,8192]{2,1,0:T(2,128)(2,1)}, u32[]{:S(2)}, u32[]{:S(2)}) %all-to-all-start) | async-done | bytes 1048608 | tf_op jit(solution)/shard_map/all_to_all | solution.py:81
  61.7 8.7 %all-to-all-start.2 = ((bf16[32,2,8192]{2,1,0:T(2,128)(2,1)}), bf16[32,2,8192]{2,1,0:T(2,128)(2,1)}, u32[]{:S(2)}, u32[]{:S(2)}) async-start(bf16[32,2,8192]{2,1,0:T(2,128)(2,1)} %reshape.268), calls=%async_computation.2 | async-start | bytes 2097152 | tf_op jit(solution)/shard_map/all_to_all | solution.py:88
  70.5 48.7 %all-gather = s32[32,1,3]{2,1,0:T(1,128)S(1)} all-gather(s32[1,1,3]{2,1,0:T(1,128)S(1)} %copy-done.32), channel_id=2, replica_groups=mesh['dp'=8,'ctx'=32] {'ctx'}, dimensions={0}, use_global_device_ids=true | all-gather | bytes 396 | tf_op jit(solution)/shard_map/all_gather | solution.py:74
  119.5 5.8 reshape.271
  127.3 2.5 gather_fusion
  129.8 5.3 all-to-all-start.1
  135.1 5.8 reshape.269
  142.9 2.6 gather_fusion.1
  145.5 54.6 %all-to-all-done.1 = bf16[32,3,16,1024]{3,2,1,0:T(8,128)(2,1)} async-done(((bf16[32,3,16,1024]{3,2,1,0:T(8,128)(2,1)}), bf16[32,3,16,1024]{3,2,1,0:T(8,128)(2,1)}, u32[]{:S(2)}, u32[]{:S(2)}) %all-to-all-start.1) | async-done | bytes 3145760 | tf_op jit(solution)/shard_map/all_to_all | solution.py:98
  200.1 5.4 all-to-all-start.3
  217.4 4.4 fusion.3
  232.8 34.6 %all-to-all-done.3 = bf16[32,3,16,1024]{3,2,1,0:T(8,128)(2,1)} async-done(((bf16[32,3,16,1024]{3,2,1,0:T(8,128)(2,1)}), bf16[32,3,16,1024]{3,2,1,0:T(8,128)(2,1)}, u32[]{:S(2)}, u32[]{:S(2)}) %all-to-all-start.3) | async-done | bytes 3145760 | tf_op jit(solution)/shard_map/all_to_all | solution.py:99
  278.4 6.3 fusion.6
  284.8 5.1 fusion.5
  289.9 5.0 fusion.4
  295.0 11.9 %divide_convert_fusion.3 = (bf16[8,512,512]{1,2,0:T(8,128)(2,1)S(1)}, bf16[8,512,512]{1,2,0:T(8,128)(2,1)S(1)}, bf16[8,512,512]{1,2,0:T(8,128)(2,1)S(1)}, bf16[8,512,512]{1,2,0:T(8,128)(2,1)S(1)}) fusion(f32[8,512,512]{1,2,0:T(8,128)S(1)} %bitcast.207, f32[8,512]{1,0:T(8,128)S(1)} %add_add_fusion.2, f32[512,512]{0,1:T(8,128)} %copy-done.14, ...), kind=kLoop, calls=%fused_computation.12 | loop fusion | flops 33554432 | bytes 51396620 | tf_op jit(solution)/shard_map/convert_element_type | solution.py:24
  306.9 2.8 fusion.41
  313.2 2.7 bitcast_convert_fusion
  315.9 2.9 copy.585
  318.8 2.5 multiply_reduce_fusion
  321.4 4.0 fusion.2
  325.5 3.3 fusion.1
  330.9 3.3 fusion
  334.2 2.5 multiply_convert_fusion.3
  336.6 6.0 copy.538
  342.6 4.6 multiply_convert_fusion.2
  347.3 6.0 copy.539
  353.3 4.6 multiply_convert_fusion.1
  358.0 6.2 copy.540
  364.1 9.6 %pad_maximum_fusion = bf16[1,3,512,1024]{3,1,0,2:T(4,128)(2,1)} fusion(bf16[1,1,512,1024]{3,1,0,2:T(2,128)(2,1)} %copy.540, bf16[1,1,512,1024]{3,1,0,2:T(2,128)(2,1)} %copy.539, bf16[1,1,512,1024]{3,1,0,2:T(2,128)(2,1)} %copy.538), kind=kLoop, calls=%fused_computation.21 | loop fusion | flops 9437184 | bytes 6291456 | tf_op jit(solution)/shard_map/stack | solution.py:126
  373.8 7.3 %all-to-all-start.4 = ((bf16[1,3,512,1024]{3,1,0,2:T(4,128)(2,1)}), bf16[1,3,512,1024]{3,1,0,2:T(4,128)(2,1)}, u32[]{:S(2)}, u32[]{:S(2)}) async-start(bf16[1,3,512,1024]{3,1,0,2:T(4,128)(2,1)} %pad_maximum_fusion), calls=%async_computation.4 | async-start | bytes 8388608 | tf_op jit(solution)/shard_map/all_to_all | solution.py:138
  381.1 4.6 convolution_convert_fusion.2
  385.7 6.1 copy.556
  391.8 4.6 convolution_convert_fusion.1
  396.4 6.0 copy.557
  402.4 4.6 convolution_convert_fusion
  407.1 6.1 copy.558
  413.2 9.7 %pad_maximum_fusion.1 = bf16[1,3,512,1024]{3,1,0,2:T(4,128)(2,1)} fusion(bf16[1,1,512,1024]{3,1,0,2:T(2,128)(2,1)} %copy.558, bf16[1,1,512,1024]{3,1,0,2:T(2,128)(2,1)} %copy.557, bf16[1,1,512,1024]{3,1,0,2:T(2,128)(2,1)} %copy.556), kind=kLoop, calls=%fused_computation.22 | loop fusion | flops 9437184 | bytes 6291456 | tf_op jit(solution)/shard_map/stack | solution.py:131
  422.9 42.1 %all-to-all-done.4 = bf16[1,3,512,1024]{3,1,0,2:T(4,128)(2,1)} async-done(((bf16[1,3,512,1024]{3,1,0,2:T(4,128)(2,1)}), bf16[1,3,512,1024]{3,1,0,2:T(4,128)(2,1)}, u32[]{:S(2)}, u32[]{:S(2)}) %all-to-all-start.4) | async-done | bytes 3145760 | tf_op jit(solution)/shard_map/all_to_all | solution.py:138
  465.0 9.8 %all-to-all-start.6 = ((bf16[1,3,512,1024]{3,1,0,2:T(4,128)(2,1)}), bf16[1,3,512,1024]{3,1,0,2:T(4,128)(2,1)}, u32[]{:S(2)}, u32[]{:S(2)}) async-start(bf16[1,3,512,1024]{3,1,0,2:T(4,128)(2,1)} %pad_maximum_fusion.1), calls=%async_computation.6 | async-start | bytes 8388608 | tf_op jit(solution)/shard_map/all_to_all | solution.py:139
  476.1 4.6 fusion.44
  480.7 3.4 copy.541
  484.5 3.6 fusion.20
  489.7 71.2 %all-to-all-done.6 = bf16[1,3,512,1024]{3,1,0,2:T(4,128)(2,1)} async-done(((bf16[1,3,512,1024]{3,1,0,2:T(4,128)(2,1)}), bf16[1,3,512,1024]{3,1,0,2:T(4,128)(2,1)}, u32[]{:S(2)}, u32[]{:S(2)}) %all-to-all-start.6) | async-done | bytes 3145760 | tf_op jit(solution)/shard_map/all_to_all | solution.py:139
  560.9 7.3 %all-to-all-start.5 = ((bf16[32,16,1024]{2,1,0:T(8,128)(2,1)}), bf16[32,16,1024]{2,1,0:T(8,128)(2,1)}, u32[]{:S(2)}, u32[]{:S(2)}) async-start(bf16[32,16,1024]{2,1,0:T(8,128)(2,1)} %copy.544), calls=%async_computation.5 | async-start | bytes 2097152 | tf_op jit(solution)/shard_map/all_to_all | solution.py:157
  568.2 3.4 fusion.45
  578.3 2.8 fusion.18
  581.0 3.4 copy.559
  584.8 3.6 fusion.23
  590.0 9.6 %all-to-all-start.7 = ((bf16[32,16,1024]{2,1,0:T(8,128)(2,1)}), bf16[32,16,1024]{2,1,0:T(8,128)(2,1)S(1)}, u32[]{:S(2)}, u32[]{:S(2)}) async-start(bf16[32,16,1024]{2,1,0:T(8,128)(2,1)} %copy.562), calls=%async_computation.7 | async-start | bytes 2097152 | tf_op jit(solution)/shard_map/all_to_all | solution.py:160
  599.6 5.0 fusion.46
  604.7 2.9 copy.563
  607.6 3.9 fusion.15
  615.0 2.8 copy.611
  617.8 3.0 copy.545
  620.9 5.2 multiply_reduce_fusion.1
  630.0 85.0 %all-reduce = (f32[128]{0:T(128)}, f32[128]{0:T(128)}) all-reduce(f32[128]{0:T(128)S(1)} %get-tuple-element.56, f32[128]{0:T(128)S(1)} %get-tuple-element.54), channel_id=1, replica_groups=mesh['dp'=8,'ctx'=32] {'dp','ctx'}, use_global_device_ids=true, to_apply=%region_9.0 | all-reduce | flops 256 | bytes 2048 | tf_op jit(solution)/shard_map/psum | solution.py:176
  (133 shorter events, 70.7 us)
Async XLA Ops:
  3.3 4.5 copy-start.31
  3.3 4.5 copy-start.26
  13.3 23.9 %copy-start.27 = (bf16[1,512,1024]{2,1,0:T(8,128)(2,1)S(1)}, bf16[1,512,1024]{2,1,0:T(8,128)(2,1)}, u32[]{:S(2)}) copy-start(bf16[1,512,1024]{2,1,0:T(8,128)(2,1)} %param.9) | copy-start | bytes 3145732
  25.0 36.8 %all-to-all-start = ((bf16[32,2,8192]{2,1,0:T(2,128)(2,1)}), bf16[32,2,8192]{2,1,0:T(2,128)(2,1)}, u32[]{:S(2)}, u32[]{:S(2)}) async-start(bf16[32,2,8192]{2,1,0:T(2,128)(2,1)} %reshape.270), calls=%async_computation | async-start | bytes 2097152 | tf_op jit(solution)/shard_map/all_to_all | solution.py:81
  40.1 30.4 %copy-start.32 = (s32[1,1,3]{2,1,0:T(1,128)S(1)}, s32[1,1,3]{2,1,0:T(1,128)}, u32[]{:S(2)}) copy-start(s32[1,1,3]{2,1,0:T(1,128)} %param.12) | copy-start | bytes 40
  61.7 68.1 %all-to-all-start.2 = ((bf16[32,2,8192]{2,1,0:T(2,128)(2,1)}), bf16[32,2,8192]{2,1,0:T(2,128)(2,1)}, u32[]{:S(2)}, u32[]{:S(2)}) async-start(bf16[32,2,8192]{2,1,0:T(2,128)(2,1)} %reshape.268), calls=%async_computation.2 | async-start | bytes 2097152 | tf_op jit(solution)/shard_map/all_to_all | solution.py:88
  129.8 70.3 %all-to-all-start.1 = ((bf16[32,3,16,1024]{3,2,1,0:T(8,128)(2,1)}), bf16[32,3,16,1024]{3,2,1,0:T(8,128)(2,1)}, u32[]{:S(2)}, u32[]{:S(2)}) async-start(bf16[32,3,16,1024]{3,2,1,0:T(8,128)(2,1)} %bitcast.215), calls=%async_computation.1 | async-start | bytes 6291456 | tf_op jit(solution)/shard_map/all_to_all | solution.py:98
  200.1 67.3 %all-to-all-start.3 = ((bf16[32,3,16,1024]{3,2,1,0:T(8,128)(2,1)}), bf16[32,3,16,1024]{3,2,1,0:T(8,128)(2,1)}, u32[]{:S(2)}, u32[]{:S(2)}) async-start(bf16[32,3,16,1024]{3,2,1,0:T(8,128)(2,1)} %bitcast.214), calls=%async_computation.3 | async-start | bytes 6291456 | tf_op jit(solution)/shard_map/all_to_all | solution.py:99
  205.5 1.9 copy-start.29
  207.4 4.2 copy-start.28
  207.4 4.5 copy-start.30
  212.1 3.2 copy-start.19
  212.1 3.2 copy-start.33
  212.8 4.5 copy-start.8
  213.0 8.8 %copy-start.14 = (f32[512,512]{0,1:T(8,128)}, f32[512,512]{0,1:T(8,128)S(1)}, u32[]{:S(2)}) copy-start(f32[512,512]{0,1:T(8,128)S(1)} %fusion.26) | copy-start | bytes 3145732
  278.4 6.3 copy-start.21
  284.8 5.1 copy-start.22
  284.8 10.1 %slice-start = ((s8[8388608]{0:T(1024)(128)(4,1)}), s8[4194304]{0:T(1024)(128)(4,1)S(1)}, s32[]{:S(2)}) async-start(s8[8388608]{0:T(1024)(128)(4,1)} %bitcast.206), calls=%async_computation.8 | async-start | bytes 8388608
  289.9 5.1 slice-start.1
  306.9 3.9 copy-start.2
  306.9 5.8 copy-start.4
  306.9 5.8 copy-start.6
  306.9 6.3 copy-start
  306.9 3.1 copy-start.15
  310.0 2.0 copy-start.17
  321.4 4.0 copy-start.5
  321.4 4.1 copy-start.16
  325.5 8.7 %copy-start.11 = (bf16[8,512,512]{1,2,0:T(8,128)(2,1)}, bf16[8,512,512]{1,2,0:T(8,128)(2,1)S(1)}, u32[]{:S(2)}) copy-start(bf16[8,512,512]{1,2,0:T(8,128)(2,1)S(1)} %fusion.2) | copy-start | bytes 12582916
  325.5 5.1 copy-start.3
  325.5 5.4 copy-start.18
  373.8 91.2 %all-to-all-start.4 = ((bf16[1,3,512,1024]{3,1,0,2:T(4,128)(2,1)}), bf16[1,3,512,1024]{3,1,0,2:T(4,128)(2,1)}, u32[]{:S(2)}, u32[]{:S(2)}) async-start(bf16[1,3,512,1024]{3,1,0,2:T(4,128)(2,1)} %pad_maximum_fusion), calls=%async_computation.4 | async-start | bytes 8388608 | tf_op jit(solution)/shard_map/all_to_all | solution.py:138
  465.0 95.9 %all-to-all-start.6 = ((bf16[1,3,512,1024]{3,1,0,2:T(4,128)(2,1)}), bf16[1,3,512,1024]{3,1,0,2:T(4,128)(2,1)}, u32[]{:S(2)}, u32[]{:S(2)}) async-start(bf16[1,3,512,1024]{3,1,0,2:T(4,128)(2,1)} %pad_maximum_fusion.1), calls=%async_computation.6 | async-start | bytes 8388608 | tf_op jit(solution)/shard_map/all_to_all | solution.py:139
  560.9 29.1 %all-to-all-start.5 = ((bf16[32,16,1024]{2,1,0:T(8,128)(2,1)}), bf16[32,16,1024]{2,1,0:T(8,128)(2,1)}, u32[]{:S(2)}, u32[]{:S(2)}) async-start(bf16[32,16,1024]{2,1,0:T(8,128)(2,1)} %copy.544), calls=%async_computation.5 | async-start | bytes 2097152 | tf_op jit(solution)/shard_map/all_to_all | solution.py:157
  568.2 3.7 copy-start.1
  572.0 1.6 copy-start.9
  572.0 3.7 copy-start.23
  573.6 2.1 copy-start.12
  573.6 3.3 copy-start.7
  573.6 4.5 copy-start.13
  573.6 4.7 copy-start.20
  590.0 125.0 %all-to-all-start.7 = ((bf16[32,16,1024]{2,1,0:T(8,128)(2,1)}), bf16[32,16,1024]{2,1,0:T(8,128)(2,1)S(1)}, u32[]{:S(2)}, u32[]{:S(2)}) async-start(bf16[32,16,1024]{2,1,0:T(8,128)(2,1)} %copy.562), calls=%async_computation.7 | async-start | bytes 2097152 | tf_op jit(solution)/shard_map/all_to_all | solution.py:160
  607.6 6.2 copy-start.25
  620.9 5.2 copy-start.10
  626.1 88.9 %copy-start.24 = (f32[1,512,1024]{2,1,0:T(8,128)S(1)}, f32[1,512,1024]{2,1,0:T(8,128)}, u32[]{:S(2)}) copy-start(f32[1,512,1024]{2,1,0:T(8,128)} %copy.563) | copy-start | bytes 6291460
where the time goes:
time: 727 us; the launch traced here: 717 us
  waiting for transfers between devices  215 us (30%)
  local copies, waits for them, and re-layouts  138 us (19%)
  blocking collectives  134 us (18%)
  matrix products  94.3 us (13%)
  other arithmetic  66.9 us (9%)
  starting transfers between devices  65.5 us (9%)
    psum x1, blocking collectives, local(): lax.psum((query_gain_part, key_gain_part), ('dp', 'ctx'))  85 us
    all_to_all x1, waiting for transfers between devices, local(): lax.all_to_all(remote_value_all, 'ctx', split_axis=2, concat_axis=0, tile...  71.2 us
    all_to_all x1, waiting for transfers between devices, local(): lax.all_to_all(holder_keys[choice_table], 'ctx', split_axis=0, concat_axi...  54.6 us
    all_gather x1, blocking collectives, local(): choice_table = lax.all_gather(selected[0], 'ctx', axis=0, tiled=True)  48.7 us
    unnamed x88, local copies, waits for them, and re-layouts  44.6 us
    all_to_all x1, waiting for transfers between devices, local(): lax.all_to_all(remote_key_all, 'ctx', split_axis=2, concat_axis=0, tiled=...  42.1 us
    all_to_all x1, waiting for transfers between devices, local(): lax.all_to_all(holder_values[choice_table], 'ctx', split_axis=0, concat_a...  34.6 us
    unnamed x5, other arithmetic  21.1 us
  transfers between devices with their start and end apart: 8, of which 5 were waited for; matrix products, arithmetic and copies ran while one was open for 23% of the time, Pallas kernels for 0%

commit v1 on v0

--- a/solution.py
+++ b/solution.py
@@ -71,7 +71,15 @@
     def heads_view(block_array):
         return block_array.reshape(block_size, head_count, head_dim)
 
-    choice_table = lax.all_gather(selected[0], "ctx", axis=0, tiled=True)
+    ways, here = (lax.axis_size("ctx"), lax.axis_index("ctx"))
+    grown, reach = (selected[0], 1)
+    while reach < ways:
+        theirs = lax.ppermute(grown, "ctx", [(d, d ^ reach) for d in range(ways)])
+        mine_first = jnp.concatenate([grown, theirs], axis=0)
+        theirs_first = jnp.concatenate([theirs, grown], axis=0)
+        grown = jnp.where(here & reach == 0, mine_first, theirs_first)
+        reach = 2 * reach
+    choice_table = grown
     query_float = query_rows[0].astype(jnp.float32)
     key_float = key_rows[0].astype(jnp.float32)
     query_normed = head_norm(query_float, query_gain).astype(jnp.bfloat16)

time: 727 us -> 741 us (1.019)
  blocking collectives: 134 us -> 79.3 us
  waiting for transfers between devices: 215 us -> 261 us
  starting transfers between devices: 65.5 us -> 87.4 us
    all_gather x1 -> x0, blocking collectives: 48.7 us -> none  [local(): choice_table = lax.all_gather(selected[0], 'ctx', axis=0, tiled=True)]
    ppermute x0 -> x5, waiting for transfers between devices: none -> 27.9 us  [local(): theirs = lax.ppermute(grown, 'ctx', [(d, d ^ reach) for d in range(ways)])]
    ppermute x0 -> x5, starting transfers between devices: none -> 21.6 us  [local(): theirs = lax.ppermute(grown, 'ctx', [(d, d ^ reach) for d in range(ways)])]
  transfers between devices with their start and end apart: 8 -> 13, of which waited for: 5 -> 10; matrix products, arithmetic and copies ran while one was open for 23% -> 22% of each run, Pallas kernels for 0% -> 0%
where the time goes in v1:
time: 741 us; the launch traced here: 731 us
  waiting for transfers between devices  261 us (35%)
  local copies, waits for them, and re-layouts  139 us (19%)
  matrix products  93.8 us (13%)
  starting transfers between devices  87.4 us (12%)
  blocking collectives  79.3 us (11%)
  other arithmetic  67 us (9%)
    psum x1, blocking collectives, local(): lax.psum((query_gain_part, key_gain_part), ('dp', 'ctx'))  79.3 us
    all_to_all x1, waiting for transfers between devices, local(): lax.all_to_all(remote_value_all, 'ctx', split_axis=2, concat_axis=0, tile...  77.9 us
    all_to_all x1, waiting for transfers between devices, local(): lax.all_to_all(holder_keys[choice_table], 'ctx', split_axis=0, concat_axi...  55.2 us
    all_to_all x1, waiting for transfers between devices, local(): lax.all_to_all(remote_key_all, 'ctx', split_axis=2, concat_axis=0, tiled=...  49.5 us
    unnamed x88, local copies, waits for them, and re-layouts  45.9 us
    all_to_all x1, waiting for transfers between devices, local(): lax.all_to_all(holder_values[choice_table], 'ctx', split_axis=0, concat_a...  38.1 us
    ppermute x5, waiting for transfers between devices, local(): theirs = lax.ppermute(grown, 'ctx', [(d, d ^ reach) for d in range(ways)])  27.9 us
    ppermute x5, starting transfers between devices, local(): theirs = lax.ppermute(grown, 'ctx', [(d, d ^ reach) for d in range(ways)])  21.6 us
  transfers between devices with their start and end apart: 13, of which 10 were waited for; matrix products, arithmetic and copies ran while one was open for 22% of the time, Pallas kernels for 0%

profile of v1, /device:TPU:1, one launch (start us, length us, event | category | flops | bytes accessed | tf_op | source)
XLA Modules:
  0.0 730.6 jit_solution(11354316170084343648)
XLA Ops:
  4.9 2.9 copy.625
  9.8 3.0 copy.663
  13.3 9.1 %reduce.3 = bf16[512,1024]{1,0:T(8,128)(2,1)} reduce(bf16[512,1,1024]{2,1,0:T(2,128)(2,1)} %bitcast.240, bf16[]{:T(256)} %broadcast.185), dimensions={1}, to_apply=%bitcast.203.reduce_sub_computation | reduce | bytes 2097154
  22.3 2.6 reshape.379
  25.0 12.3 %all-to-all-start = ((bf16[32,2,8192]{2,1,0:T(2,128)(2,1)}), bf16[32,2,8192]{2,1,0:T(2,128)(2,1)}, u32[]{:S(2)}, u32[]{:S(2)}) async-start(bf16[32,2,8192]{2,1,0:T(2,128)(2,1)} %reshape.379), calls=%async_computation | async-start | bytes 2097152 | tf_op jit(solution)/shard_map/all_to_all | solution.py:89
  37.2 3.0 copy.662
  40.2 8.0 %reduce.2 = bf16[512,1024]{1,0:T(8,128)(2,1)S(1)} reduce(bf16[512,1,1024]{2,1,0:T(2,128)(2,1)} %bitcast.241, bf16[]{:T(256)} %broadcast.185), dimensions={1}, to_apply=%bitcast.202.reduce_sub_computation | reduce | bytes 2097154
  49.8 12.0 %all-to-all-done = bf16[32,2,8192]{2,1,0:T(2,128)(2,1)} async-done(((bf16[32,2,8192]{2,1,0:T(2,128)(2,1)}), bf16[32,2,8192]{2,1,0:T(2,128)(2,1)}, u32[]{:S(2)}, u32[]{:S(2)}) %all-to-all-start) | async-done | bytes 1048608 | tf_op jit(solution)/shard_map/all_to_all | solution.py:89
  61.8 8.7 %all-to-all-start.2 = ((bf16[32,2,8192]{2,1,0:T(2,128)(2,1)}), bf16[32,2,8192]{2,1,0:T(2,128)(2,1)}, u32[]{:S(2)}, u32[]{:S(2)}) async-start(bf16[32,2,8192]{2,1,0:T(2,128)(2,1)} %reshape.377), calls=%async_computation.2 | async-start | bytes 2097152 | tf_op jit(solution)/shard_map/all_to_all | solution.py:96
  71.8 21.3 %collective-permute-done = s32[1,3]{1,0:T(1,128)S(1)} collective-permute-done((s32[1,3]{1,0:T(1,128)S(1)}, s32[1,3]{1,0:T(1,128)S(1)}, u32[]{:S(2)}, u32[]{:S(2)}) %collective-permute-start) | collective-permute-done | bytes 44 | tf_op jit(solution)/shard_map/ppermute | solution.py:77
  96.9 4.5 collective-permute-start.2
  106.3 12.8 %collective-permute-start.4 = (s32[16,3]{0,1:T(4,128)S(1)}, s32[16,3]{0,1:T(4,128)S(1)}, u32[]{:S(2)}, u32[]{:S(2)}) collective-permute-start(s32[16,3]{0,1:T(4,128)S(1)} %add_select_fusion.2), channel_id=1, source_target_pairs={{0,16},{1,17},{2,18},{3,19},{4,20},{5,21},{6,22},{7,23},{8,24},{9,... | collective-permute-start | bytes 584 | tf_op jit(solution)/shard_map/ppermute | solution.py:77
  120.6 5.8 reshape.380
  130.9 8.0 %all-to-all-start.1 = ((bf16[32,3,16,1024]{3,2,1,0:T(8,128)(2,1)}), bf16[32,3,16,1024]{3,2,1,0:T(8,128)(2,1)}, u32[]{:S(2)}, u32[]{:S(2)}) async-start(bf16[32,3,16,1024]{3,2,1,0:T(8,128)(2,1)} %bitcast.218), calls=%async_computation.1 | async-start | bytes 6291456 | tf_op jit(solution)/shard_map/all_to_all | solution.py:106
  138.8 5.8 reshape.378
  146.6 2.6 gather_fusion.1
  149.2 55.2 %all-to-all-done.1 = bf16[32,3,16,1024]{3,2,1,0:T(8,128)(2,1)} async-done(((bf16[32,3,16,1024]{3,2,1,0:T(8,128)(2,1)}), bf16[32,3,16,1024]{3,2,1,0:T(8,128)(2,1)}, u32[]{:S(2)}, u32[]{:S(2)}) %all-to-all-start.1) | async-done | bytes 3145760 | tf_op jit(solution)/shard_map/all_to_all | solution.py:106
  204.3 7.6 %all-to-all-start.3 = ((bf16[32,3,16,1024]{3,2,1,0:T(8,128)(2,1)}), bf16[32,3,16,1024]{3,2,1,0:T(8,128)(2,1)}, u32[]{:S(2)}, u32[]{:S(2)}) async-start(bf16[32,3,16,1024]{3,2,1,0:T(8,128)(2,1)} %bitcast.217), calls=%async_computation.3 | async-start | bytes 6291456 | tf_op jit(solution)/shard_map/all_to_all | solution.py:107
  223.9 4.5 fusion.3
  239.4 38.1 %all-to-all-done.3 = bf16[32,3,16,1024]{3,2,1,0:T(8,128)(2,1)} async-done(((bf16[32,3,16,1024]{3,2,1,0:T(8,128)(2,1)}), bf16[32,3,16,1024]{3,2,1,0:T(8,128)(2,1)}, u32[]{:S(2)}, u32[]{:S(2)}) %all-to-all-start.3) | async-done | bytes 3145760 | tf_op jit(solution)/shard_map/all_to_all | solution.py:107
  288.6 6.3 fusion.6
  294.9 5.1 fusion.5
  300.1 5.1 fusion.4
  305.1 11.8 %divide_convert_fusion.3 = (bf16[8,512,512]{1,2,0:T(8,128)(2,1)S(1)}, bf16[8,512,512]{1,2,0:T(8,128)(2,1)S(1)}, bf16[8,512,512]{1,2,0:T(8,128)(2,1)S(1)}, bf16[8,512,512]{1,2,0:T(8,128)(2,1)S(1)}) fusion(f32[8,512,512]{1,2,0:T(8,128)S(1)} %bitcast.210, f32[8,512]{1,0:T(8,128)S(1)} %add_add_fusion.2, f32[512,512]{0,1:T(8,128)} %copy-done.15, ...), kind=kLoop, calls=%fused_computation.12 | loop fusion | flops 33554432 | bytes 51396620 | tf_op jit(solution)/shard_map/convert_element_type | solution.py:24
  317.0 2.8 fusion.41
  323.3 2.7 bitcast_convert_fusion
  326.1 2.9 copy.608
  331.6 4.0 fusion.2
  335.6 3.3 fusion.1
  341.0 3.3 fusion
  346.8 6.0 copy.561
  352.8 4.6 multiply_convert_fusion.2
  357.4 6.0 copy.562
  363.5 4.6 multiply_convert_fusion.1
  368.1 6.1 copy.563
  374.2 9.6 %pad_maximum_fusion = bf16[1,3,512,1024]{3,1,0,2:T(4,128)(2,1)} fusion(bf16[1,1,512,1024]{3,1,0,2:T(2,128)(2,1)} %copy.563, bf16[1,1,512,1024]{3,1,0,2:T(2,128)(2,1)} %copy.562, bf16[1,1,512,1024]{3,1,0,2:T(2,128)(2,1)} %copy.561), kind=kLoop, calls=%fused_computation.21 | loop fusion | flops 9437184 | bytes 6291456 | tf_op jit(solution)/shard_map/stack | solution.py:134
  383.9 7.5 %all-to-all-start.4 = ((bf16[1,3,512,1024]{3,1,0,2:T(4,128)(2,1)}), bf16[1,3,512,1024]{3,1,0,2:T(4,128)(2,1)}, u32[]{:S(2)}, u32[]{:S(2)}) async-start(bf16[1,3,512,1024]{3,1,0,2:T(4,128)(2,1)} %pad_maximum_fusion), calls=%async_computation.4 | async-start | bytes 8388608 | tf_op jit(solution)/shard_map/all_to_all | solution.py:146
  391.4 4.6 convolution_convert_fusion.2
  396.0 6.0 copy.579
  402.1 4.6 convolution_convert_fusion.1
  406.7 6.1 copy.580
  412.7 4.6 convolution_convert_fusion
  417.4 6.0 copy.581
  423.4 9.7 %pad_maximum_fusion.1 = bf16[1,3,512,1024]{3,1,0,2:T(4,128)(2,1)} fusion(bf16[1,1,512,1024]{3,1,0,2:T(2,128)(2,1)} %copy.581, bf16[1,1,512,1024]{3,1,0,2:T(2,128)(2,1)} %copy.580, bf16[1,1,512,1024]{3,1,0,2:T(2,128)(2,1)} %copy.579), kind=kLoop, calls=%fused_computation.22 | loop fusion | flops 9437184 | bytes 6291456 | tf_op jit(solution)/shard_map/stack | solution.py:139
  433.1 49.5 %all-to-all-done.4 = bf16[1,3,512,1024]{3,1,0,2:T(4,128)(2,1)} async-done(((bf16[1,3,512,1024]{3,1,0,2:T(4,128)(2,1)}), bf16[1,3,512,1024]{3,1,0,2:T(4,128)(2,1)}, u32[]{:S(2)}, u32[]{:S(2)}) %all-to-all-start.4) | async-done | bytes 3145760 | tf_op jit(solution)/shard_map/all_to_all | solution.py:146
  482.6 4.9 all-to-all-start.6
  487.8 4.6 fusion.44
  492.4 3.4 copy.564
  496.1 3.6 fusion.20
  501.3 77.9 %all-to-all-done.6 = bf16[1,3,512,1024]{3,1,0,2:T(4,128)(2,1)} async-done(((bf16[1,3,512,1024]{3,1,0,2:T(4,128)(2,1)}), bf16[1,3,512,1024]{3,1,0,2:T(4,128)(2,1)}, u32[]{:S(2)}, u32[]{:S(2)}) %all-to-all-start.6) | async-done | bytes 3145760 | tf_op jit(solution)/shard_map/all_to_all | solution.py:147
  579.2 7.2 all-to-all-start.5
  586.4 3.4 fusion.45
  596.5 2.8 fusion.18
  599.2 3.4 copy.582
  603.0 3.6 fusion.23
  608.2 9.7 %all-to-all-start.7 = ((bf16[32,16,1024]{2,1,0:T(8,128)(2,1)}), bf16[32,16,1024]{2,1,0:T(8,128)(2,1)}, u32[]{:S(2)}, u32[]{:S(2)}) async-start(bf16[32,16,1024]{2,1,0:T(8,128)(2,1)} %copy.585), calls=%async_computation.7 | async-start | bytes 2097152 | tf_op jit(solution)/shard_map/all_to_all | solution.py:168
  617.9 5.1 fusion.46
  623.0 3.1 copy.586
  626.1 3.2 fusion.15
  633.8 3.0 copy.634
  636.8 2.9 copy.568
  639.7 4.5 multiply_reduce_fusion.1
  648.2 79.3 %all-reduce = (f32[128]{0:T(128)}, f32[128]{0:T(128)}) all-reduce(f32[128]{0:T(128)S(1)} %get-tuple-element.56, f32[128]{0:T(128)S(1)} %get-tuple-element.54), channel_id=1, replica_groups=mesh['dp'=8,'ctx'=32] {'dp','ctx'}, use_global_device_ids=true, to_apply=%region_9.10 | all-reduce | flops 256 | bytes 2048 | tf_op jit(solution)/shard_map/psum | solution.py:184
  727.6 2.5 fusion.17
  (147 shorter events, 88.0 us)
Async XLA Ops:
  3.3 4.5 copy-start.31
  3.3 4.5 copy-start.26
  13.3 24.0 %copy-start.27 = (bf16[1,512,1024]{2,1,0:T(8,128)(2,1)S(1)}, bf16[1,512,1024]{2,1,0:T(8,128)(2,1)}, u32[]{:S(2)}) copy-start(bf16[1,512,1024]{2,1,0:T(8,128)(2,1)} %param.9) | copy-start | bytes 3145732
  25.0 36.9 %all-to-all-start = ((bf16[32,2,8192]{2,1,0:T(2,128)(2,1)}), bf16[32,2,8192]{2,1,0:T(2,128)(2,1)}, u32[]{:S(2)}, u32[]{:S(2)}) async-start(bf16[32,2,8192]{2,1,0:T(2,128)(2,1)} %reshape.379), calls=%async_computation | async-start | bytes 2097152 | tf_op jit(solution)/shard_map/all_to_all | solution.py:89
  40.2 30.4 %copy-start.32 = (s32[1,1,3]{2,1,0:T(1,128)S(1)}, s32[1,1,3]{2,1,0:T(1,128)}, u32[]{:S(2)}) copy-start(s32[1,1,3]{2,1,0:T(1,128)} %param.12) | copy-start | bytes 40
  61.8 69.0 %all-to-all-start.2 = ((bf16[32,2,8192]{2,1,0:T(2,128)(2,1)}), bf16[32,2,8192]{2,1,0:T(2,128)(2,1)}, u32[]{:S(2)}, u32[]{:S(2)}) async-start(bf16[32,2,8192]{2,1,0:T(2,128)(2,1)} %reshape.377), calls=%async_computation.2 | async-start | bytes 2097152 | tf_op jit(solution)/shard_map/all_to_all | solution.py:96
  70.5 22.5 %collective-permute-start = (s32[1,3]{1,0:T(1,128)S(1)}, s32[1,3]{1,0:T(1,128)S(1)}, u32[]{:S(2)}, u32[]{:S(2)}) collective-permute-start(s32[1,3]{1,0:T(1,128)S(1)} %bitcast.258), channel_id=1, source_target_pairs={{0,1},{1,0},{2,3},{3,2},{4,5},{5,4},{6,7},{7,6},{8,9},{9,8},{10,11... | collective-permute-start | bytes 44 | tf_op jit(solution)/shard_map/ppermute | solution.py:77
  93.1 3.8 collective-permute-start.1
  96.9 6.4 collective-permute-start.2
  103.3 2.8 collective-permute-start.3
  106.3 14.0 %collective-permute-start.4 = (s32[16,3]{0,1:T(4,128)S(1)}, s32[16,3]{0,1:T(4,128)S(1)}, u32[]{:S(2)}, u32[]{:S(2)}) collective-permute-start(s32[16,3]{0,1:T(4,128)S(1)} %add_select_fusion.2), channel_id=1, source_target_pairs={{0,16},{1,17},{2,18},{3,19},{4,20},{5,21},{6,22},{7,23},{8,24},{9,... | collective-permute-start | bytes 584 | tf_op jit(solution)/shard_map/ppermute | solution.py:77
  130.9 73.5 %all-to-all-start.1 = ((bf16[32,3,16,1024]{3,2,1,0:T(8,128)(2,1)}), bf16[32,3,16,1024]{3,2,1,0:T(8,128)(2,1)}, u32[]{:S(2)}, u32[]{:S(2)}) async-start(bf16[32,3,16,1024]{3,2,1,0:T(8,128)(2,1)} %bitcast.218), calls=%async_computation.1 | async-start | bytes 6291456 | tf_op jit(solution)/shard_map/all_to_all | solution.py:106
  204.3 73.3 %all-to-all-start.3 = ((bf16[32,3,16,1024]{3,2,1,0:T(8,128)(2,1)}), bf16[32,3,16,1024]{3,2,1,0:T(8,128)(2,1)}, u32[]{:S(2)}, u32[]{:S(2)}) async-start(bf16[32,3,16,1024]{3,2,1,0:T(8,128)(2,1)} %bitcast.217), calls=%async_computation.3 | async-start | bytes 6291456 | tf_op jit(solution)/shard_map/all_to_all | solution.py:107
  212.0 1.9 copy-start.29
  213.9 4.2 copy-start.28
  213.9 4.5 copy-start.30
  218.7 3.2 copy-start.20
  218.7 3.2 copy-start.33
  219.4 4.5 copy-start.9
  219.5 8.9 %copy-start.15 = (f32[512,512]{0,1:T(8,128)}, f32[512,512]{0,1:T(8,128)S(1)}, u32[]{:S(2)}) copy-start(f32[512,512]{0,1:T(8,128)S(1)} %fusion.26) | copy-start | bytes 3145732
  288.6 6.3 copy-start.22
  294.9 5.1 copy-start.23
  294.9 10.2 %slice-start = ((s8[8388608]{0:T(1024)(128)(4,1)}), s8[4194304]{0:T(1024)(128)(4,1)S(1)}, s32[]{:S(2)}) async-start(s8[8388608]{0:T(1024)(128)(4,1)} %bitcast.209), calls=%async_computation.8 | async-start | bytes 8388608
  300.1 5.1 slice-start.1
  317.0 3.9 copy-start.2
  317.0 5.8 copy-start.4
  317.0 5.8 copy-start.6
  317.0 6.3 copy-start
  317.0 3.1 copy-start.16
  320.1 2.0 copy-start.18
  331.6 4.0 copy-start.5
  331.6 4.1 copy-start.17
  335.6 8.7 %copy-start.12 = (bf16[8,512,512]{1,2,0:T(8,128)(2,1)}, bf16[8,512,512]{1,2,0:T(8,128)(2,1)S(1)}, u32[]{:S(2)}) copy-start(bf16[8,512,512]{1,2,0:T(8,128)(2,1)S(1)} %fusion.2) | copy-start | bytes 12582916
  335.6 5.1 copy-start.3
  335.6 5.4 copy-start.19
  383.9 98.8 %all-to-all-start.4 = ((bf16[1,3,512,1024]{3,1,0,2:T(4,128)(2,1)}), bf16[1,3,512,1024]{3,1,0,2:T(4,128)(2,1)}, u32[]{:S(2)}, u32[]{:S(2)}) async-start(bf16[1,3,512,1024]{3,1,0,2:T(4,128)(2,1)} %pad_maximum_fusion), calls=%async_computation.4 | async-start | bytes 8388608 | tf_op jit(solution)/shard_map/all_to_all | solution.py:146
  482.6 96.6 %all-to-all-start.6 = ((bf16[1,3,512,1024]{3,1,0,2:T(4,128)(2,1)}), bf16[1,3,512,1024]{3,1,0,2:T(4,128)(2,1)}, u32[]{:S(2)}, u32[]{:S(2)}) async-start(bf16[1,3,512,1024]{3,1,0,2:T(4,128)(2,1)} %pad_maximum_fusion.1), calls=%async_computation.6 | async-start | bytes 8388608 | tf_op jit(solution)/shard_map/all_to_all | solution.py:147
  579.2 28.9 %all-to-all-start.5 = ((bf16[32,16,1024]{2,1,0:T(8,128)(2,1)}), bf16[32,16,1024]{2,1,0:T(8,128)(2,1)}, u32[]{:S(2)}, u32[]{:S(2)}) async-start(bf16[32,16,1024]{2,1,0:T(8,128)(2,1)} %copy.567), calls=%async_computation.5 | async-start | bytes 2097152 | tf_op jit(solution)/shard_map/all_to_all | solution.py:165
  586.4 3.7 copy-start.1
  590.2 1.6 copy-start.10
  590.2 3.7 copy-start.24
  591.8 2.1 copy-start.13
  591.8 3.3 copy-start.7
  591.8 4.5 copy-start.14
  591.8 4.7 copy-start.21
  608.2 119.4 %all-to-all-start.7 = ((bf16[32,16,1024]{2,1,0:T(8,128)(2,1)}), bf16[32,16,1024]{2,1,0:T(8,128)(2,1)}, u32[]{:S(2)}, u32[]{:S(2)}) async-start(bf16[32,16,1024]{2,1,0:T(8,128)(2,1)} %copy.585), calls=%async_computation.7 | async-start | bytes 2097152 | tf_op jit(solution)/shard_map/all_to_all | solution.py:168
  623.0 3.1 copy-start.8
  633.8 5.9 copy-start.11
  645.8 81.8 %copy-start.25 = (f32[1,512,1024]{2,1,0:T(8,128)S(1)}, f32[1,512,1024]{2,1,0:T(8,128)}, u32[]{:S(2)}) copy-start(f32[1,512,1024]{2,1,0:T(8,128)} %copy.586) | copy-start | bytes 6291460
